TPU v7x, 128 devices: a whole 4x4x4 slice. The times are simulated.
128 devices in a mesh: side: 2 (over core), grp: 8 (over x_hi, y), tp: 8 (over x_lo, z).
Axes of the slice: x: 4 (x_hi: 2, x_lo: 2; x = x_hi * 2 + x_lo), y: 4, z: 4, core: 2. Of those that a mesh axis runs over, the one named last changes fastest.
Arguments:
- queries: bfloat16 [192, 4096], P('grp', 'side'), may hold values from -6 to 6
- kv_cache: bfloat16 [192, 16, 192, 256], P('grp', ('side', 'tp')), may hold values from -6 to 6
- lengths: int32 [192], P('grp'), may hold values from 2 to 768, as said below
- out_weight: bfloat16 [4096, 2048], P(('side', 'tp')), may hold values from -1 to 1
- resid: bfloat16 [192, 2048], P('grp'), may hold values from -6 to 6
- norm_gain: float32 [2048], replicated, may hold values from 0.1 to 1.9
- expert_ids: int32 [192, 8], P('grp'), may hold values from 0 to 127, all different within a row; in each aligned block of 24 rows (0 to 23, 24 to 47, ...) at most 3 rows name the same one
- expert_gates: float32 [192, 8], P('grp'), may hold values from 0.05 to 1
- w_gate_up: bfloat16 [128, 2048, 1536], P(('side', 'grp', 'tp')), may hold values from -0.125 to 0.125
- w_down: bfloat16 [128, 768, 2048], P(('side', 'grp', 'tp')), may hold values from -0.21875 to 0.21875
Outputs:
- layer_out: bfloat16 [192, 2048], P('grp', ('side', 'tp'))
Inputs may be any that keep to these rules, and one draw needn't show every extreme that they name: `lengths`: every row's cache holds at least two tokens; some row holds exactly 768. `expert_ids`: each row names 8 different experts. Among the rows of one row group no expert is named by more than 3 rows; in some group an expert is named by exactly 3.
All inputs are finite; a program needn't handle non-finite values.
Results may differ from a plain program's by a relative error of at most 0.017.
Values may be sent and summed in bfloat16 or wider, within the bound.
A program may use at most 64 MiB of HBM per device.

v0:
```python
import math

import jax
import jax.numpy as jnp
from jax import lax
from jax.sharding import PartitionSpec as P

QH = 32
KVH = 4
HD = 128
TOPK = 8


def swapped(value, axis, distance):
    mask = 2**distance
    pairs = [(source, source ^ mask) for source in range(lax.axis_size(axis))]
    return lax.ppermute(value, axis, pairs)


def body(
    queries,
    kv_cache,
    lengths,
    out_weight,
    resid,
    norm_gain,
    expert_ids,
    expert_gates,
    w_gate_up,
    w_down,
):
    lane_count = lax.axis_size("tp")
    tp_index = lax.axis_index("tp")
    side_count = lax.axis_size("side")
    section = lax.axis_index("side")
    grp_count = lax.axis_size("grp")
    group_size = side_count * lane_count
    member_index = section * lane_count + tp_index
    kv_parts = group_size // KVH
    group_heads = QH // KVH
    per_member = QH // group_size
    part_span = kv_cache.shape[2]
    model_width = out_weight.shape[1]
    piece_width = model_width // group_size
    rows_grp = lengths.shape[0]
    local_experts = w_gate_up.shape[0]
    experts_all = local_experts * side_count * grp_count * lane_count
    capacity = max(2, 2 * rows_grp * TOPK // experts_all)
    head_start = tp_index // kv_parts * group_heads * HD
    part_index = tp_index % kv_parts
    row_count = queries.shape[0]
    query_rows = lax.dynamic_slice_in_dim(queries, head_start, group_heads * HD, 1).reshape(
        row_count, group_heads, HD
    )
    key_rows = kv_cache[:, 0, :, :HD]
    value_rows = kv_cache[:, 0, :, HD:]
    positions = part_index * part_span + jnp.arange(part_span, dtype=jnp.int32)
    valid_mask = (positions[None, :] < lengths[:, None])[:, None, :]
    scores = jnp.einsum(
        "rgd,rpd->rgp", query_rows, key_rows, preferred_element_type=jnp.float32
    ) / math.sqrt(HD)
    scores = jnp.where(valid_mask, scores, -1e30)
    row_max = jnp.max(scores, axis=-1)
    for bit_index in range(kv_parts.bit_length() - 1):
        row_max = jnp.maximum(row_max, swapped(row_max, "tp", bit_index))
    weights = jnp.where(valid_mask, jnp.exp(scores - row_max[..., None]), 0.0)
    weight_sum = jnp.sum(weights, axis=-1)
    numerator = jnp.einsum(
        "rgp,rpd->rgd", weights.astype(jnp.bfloat16), value_rows, preferred_element_type=jnp.float32
    )
    for bit_index in range(kv_parts.bit_length() - 1):
        other_numerator, other_sum = swapped((numerator, weight_sum), "tp", bit_index)
        numerator = numerator + other_numerator
        weight_sum = weight_sum + other_sum
    heads_out = (numerator / weight_sum[..., None]).astype(jnp.bfloat16)
    mine = lax.dynamic_slice_in_dim(heads_out, part_index * per_member, per_member, 1).reshape(
        row_count, per_member * HD
    )
    projected = jnp.dot(mine, out_weight, preferred_element_type=jnp.float32)
    summed = lax.psum(projected, ("side", "tp"))
    middle = (resid.astype(jnp.float32) + summed).astype(jnp.bfloat16)
    middle_wide = middle.astype(jnp.float32)
    inv_rms = lax.rsqrt(jnp.mean(middle_wide * middle_wide, axis=-1, keepdims=True) + 1e-06)
    normed = (middle_wide * inv_rms * norm_gain).astype(jnp.bfloat16)
    column_experts = (
        (
            (section * grp_count + jnp.arange(grp_count, dtype=jnp.int32)[:, None]) * lane_count
            + tp_index
        )
        * local_experts
        + jnp.arange(local_experts, dtype=jnp.int32)[None, :]
    ).reshape(-1)
    matches = expert_ids[:, :, None] == column_experts[None, None, :]
    hit_count = jnp.sum(matches.astype(jnp.int32), axis=1)
    gate_cols = jnp.sum(jnp.where(matches, expert_gates[:, :, None], 0.0), axis=1)
    slot_rank = jnp.cumsum(hit_count, axis=0) - hit_count
    slot_ids = jnp.arange(capacity, dtype=jnp.int32)
    placed = (hit_count[:, :, None] == 1) & (slot_rank[:, :, None] == slot_ids[None, None, :])
    send_map = placed.astype(jnp.bfloat16)
    outgoing = jnp.einsum(
        "rcs,rd->csd", send_map, normed, preferred_element_type=jnp.float32
    ).astype(jnp.bfloat16)
    outgoing = outgoing.reshape(grp_count, local_experts, capacity, model_width)
    hidden = jnp.einsum(
        "gjcd,jdf->gjcf",
        lax.all_to_all(outgoing, "grp", split_axis=0, concat_axis=0, tiled=True),
        w_gate_up,
        preferred_element_type=jnp.float32,
    )
    inner_width = hidden.shape[-1] // 2
    activated = (jax.nn.silu(hidden[..., :inner_width]) * hidden[..., inner_width:]).astype(
        jnp.bfloat16
    )
    produced = jnp.einsum(
        "gjcf,jfd->gjcd", activated, w_down, preferred_element_type=jnp.float32
    ).astype(jnp.bfloat16)
    returned = lax.all_to_all(produced, "grp", split_axis=0, concat_axis=0, tiled=True)
    combine_weights = (send_map.astype(jnp.float32) * gate_cols[:, :, None]).reshape(row_count, -1)
    moe_part = jnp.dot(
        combine_weights,
        returned.reshape(-1, model_width).astype(jnp.float32),
        precision=lax.Precision.HIGHEST,
    )
    middle_mine = lax.dynamic_slice_in_dim(middle_wide, member_index * piece_width, piece_width, 1)
    moe_whole = lax.psum(moe_part, ("side", "tp"))
    return (
        middle_mine
        + lax.dynamic_slice_in_dim(moe_whole, member_index * piece_width, piece_width, 1)
    ).astype(jnp.bfloat16)


def solution(mesh):
    in_specs = (
        P("grp", "side"),
        P("grp", ("side", "tp"), None, None),
        P("grp"),
        P(("side", "tp"), None),
        P("grp", None),
        P(),
        P("grp", None),
        P("grp", None),
        P(("side", "grp", "tp"), None, None),
        P(("side", "grp", "tp"), None, None),
    )
    out_specs = P("grp", ("side", "tp"))
    return jax.shard_map(body, mesh=mesh, in_specs=in_specs, out_specs=out_specs, check_vma=False)
```

profile of v0, /device:TPU:1, one launch (start us, length us, event | category | flops | bytes accessed | tf_op | source)
XLA Modules:
  0.0 333.3 jit_solution(7118665528007655057)
XLA Ops:
  6.6 1.0 dynamic-slice_bitcast_fusion
  8.3 2.1 fusion.47
  10.3 2.5 collective-permute-start
  12.8 0.8 fusion.34
  13.9 3.4 %collective-permute-start.1 = (f32[24,8]{1,0:T(8,128)S(1)}, f32[24,8]{1,0:T(8,128)S(1)}, u32[]{:S(2)}, u32[]{:S(2)}) collective-permute-start(f32[24,8]{1,0:T(8,128)S(1)} %max.6), channel_id=1, source_target_pairs={{0,2},{1,3},{2,0},{3,1},{4,6},{5,7},{6,4},{7,5},{8,10},{9,11},{10,... | collective-permute-start | bytes 2312 | tf_op jit(solution)/shard_map/ppermute | solution.py:17
  18.7 1.0 collective-permute-start.4
  19.7 1.7 fusion.14
  22.0 2.9 collective-permute-start.5
  24.9 0.8 fusion.35
  25.9 1.1 collective-permute-done.5
  27.0 2.0 collective-permute-start.3
  29.1 2.9 collective-permute-done.3
  32.2 2.2 fusion.39
  34.4 1.3 convert_multiply_fusion
  35.7 130.8 %all-reduce.3.cloned.1.call-done = f32[24,2048]{1,0:T(8,128)} async-done(((f32[24,2048]{1,0:T(8,128)}), f32[24,2048]{1,0:T(8,128)}) %all-reduce.3.cloned.1.call-update) | async-done | bytes 196624 | tf_op jit(solution)/shard_map/psum | solution.py:80
  166.5 1.1 multiply_reduce_fusion
  167.5 0.9 fusion.10
  168.6 13.4 %all_to_all.10 = bf16[8,1,3,2048]{3,2,1,0:T(4,128)(2,1)S(1)} all-to-all(bf16[8,1,3,2048]{3,2,1,0:T(4,128)(2,1)S(1)} %copy.41), channel_id=1, replica_groups=mesh['side'=2,'grp'=8,'tp'=8] {'grp'}, dimensions={0} | all-to-all | bytes 196608 | tf_op jit(solution)/shard_map/all_to_all | solution.py:106
  182.0 3.7 %fusion.4 = f32[8,1,3,1536]{3,0,2,1:T(8,128)S(1)} fusion(bf16[1,2048,1536]{2,1,0:T(8,128)(2,1)} %param.18, bf16[8,1,3,2048]{3,2,1,0:T(4,128)(2,1)S(1)} %all_to_all.10), kind=kOutput, calls=%fused_computation.4 | convolution fusion | flops 150994944 | bytes 6537216 | tf_op jit(solution)/shard_map/gjcd,jdf->gjcf/dot_general | solution.py:104
  187.0 3.4 %all-to-all-start.1 = ((bf16[8,1,3,2048]{3,2,1,0:T(4,128)(2,1)}), bf16[8,1,3,2048]{3,2,1,0:T(4,128)(2,1)S(1)}, u32[]{:S(2)}, u32[]{:S(2)}) async-start(bf16[8,1,3,2048]{3,2,1,0:T(4,128)(2,1)} %copy.43), calls=%async_computation.1 | async-start | bytes 262144 | tf_op jit(solution)/shard_map/all_to_all | solution.py:117
  190.4 6.8 %all-to-all-done.1 = bf16[8,1,3,2048]{3,2,1,0:T(4,128)(2,1)S(1)} async-done(((bf16[8,1,3,2048]{3,2,1,0:T(4,128)(2,1)}), bf16[8,1,3,2048]{3,2,1,0:T(4,128)(2,1)S(1)}, u32[]{:S(2)}, u32[]{:S(2)}) %all-to-all-start.1) | async-done | bytes 98336 | tf_op jit(solution)/shard_map/all_to_all | solution.py:117
  197.9 1.9 fusion.48
  199.8 125.3 %all-reduce.5.cloned.1.call-done = f32[24,2048]{1,0:T(8,128)} async-done(((f32[24,2048]{1,0:T(8,128)}), f32[24,2048]{1,0:T(8,128)}) %all-reduce.5.cloned.1.call-update) | async-done | bytes 196624 | tf_op jit(solution)/shard_map/psum | solution.py:125
  325.1 1.3 add_convert_fusion.1
  (40 shorter events, 5.5 us)
Async XLA Ops:
  6.5 179.2 %copy-start = (bf16[1,768,2048]{2,1,0:T(8,128)(2,1)S(1)}, bf16[1,768,2048]{2,1,0:T(8,128)(2,1)}, u32[]{:S(2)}) copy-start(bf16[1,768,2048]{2,1,0:T(8,128)(2,1)} %param.19) | copy-start | bytes 9437188
  6.5 18.4 %copy-start.3 = (s32[24,8]{0,1:T(8,128)S(1)}, s32[24,8]{0,1:T(8,128)}, u32[]{:S(2)}) copy-start(s32[24,8]{0,1:T(8,128)} %param.16) | copy-start | bytes 2308
  6.5 159.9 %all-reduce.3.cloned.1.call-start = ((), (), s32[]{:S(2)}) async-start(), calls=%async_computation.2 | async-start | bytes 393216 | tf_op jit(solution)/shard_map/psum | solution.py:80
  8.3 158.2 %copy-start.1 = (bf16[24,2048]{1,0:T(8,128)(2,1)S(1)}, bf16[24,2048]{1,0:T(8,128)(2,1)}, u32[]{:S(2)}) copy-start(bf16[24,2048]{1,0:T(8,128)(2,1)} %param.14) | copy-start | bytes 294916
  10.3 3.6 %collective-permute-start = (f32[24,8]{1,0:T(8,128)S(1)}, f32[24,8]{1,0:T(8,128)S(1)}, u32[]{:S(2)}, u32[]{:S(2)}) collective-permute-start(f32[24,8]{1,0:T(8,128)S(1)} %get-tuple-element.9), channel_id=1, source_target_pairs={{0,1},{1,0},{2,3},{3,2},{4,5},{5,4},{6,7},{7,6},{8,9},{9,8},{10,11... | collective-permute-start | bytes 2312 | tf_op jit(solution)/shard_map/ppermute | solution.py:17
  13.9 4.6 %collective-permute-start.1 = (f32[24,8]{1,0:T(8,128)S(1)}, f32[24,8]{1,0:T(8,128)S(1)}, u32[]{:S(2)}, u32[]{:S(2)}) collective-permute-start(f32[24,8]{1,0:T(8,128)S(1)} %max.6), channel_id=1, source_target_pairs={{0,2},{1,3},{2,0},{3,1},{4,6},{5,7},{6,4},{7,5},{8,10},{9,11},{10,... | collective-permute-start | bytes 2312 | tf_op jit(solution)/shard_map/ppermute | solution.py:17
  18.7 3.3 collective-permute-start.4
  21.4 5.6 %collective-permute-start.2 = (f32[24,8,128]{2,1,0:T(8,128)S(1)}, f32[24,8,128]{2,1,0:T(8,128)S(1)}, u32[]{:S(2)}, u32[]{:S(2)}) collective-permute-start(f32[24,8,128]{2,1,0:T(8,128)S(1)} %fusion.14), channel_id=1, source_target_pairs={{0,1},{1,0},{2,3},{3,2},{4,5},{5,4},{6,7},{7,6},{8,9},{9,8},{10,11... | collective-permute-start | bytes 294920 | tf_op jit(solution)/shard_map/ppermute | solution.py:17
  22.0 5.0 %collective-permute-start.5 = (f32[24,8]{1,0:T(8,128)S(1)}, f32[24,8]{1,0:T(8,128)S(1)}, u32[]{:S(2)}, u32[]{:S(2)}) collective-permute-start(f32[24,8]{1,0:T(8,128)S(1)} %add.92), channel_id=1, source_target_pairs={{0,2},{1,3},{2,0},{3,1},{4,6},{5,7},{6,4},{7,5},{8,10},{9,11},{10,... | collective-permute-start | bytes 2312 | tf_op jit(solution)/shard_map/ppermute | solution.py:17
  27.0 5.1 %collective-permute-start.3 = (f32[24,8,128]{2,1,0:T(8,128)S(1)}, f32[24,8,128]{2,1,0:T(8,128)S(1)}, u32[]{:S(2)}, u32[]{:S(2)}) collective-permute-start(f32[24,8,128]{2,1,0:T(8,128)S(1)} %add.90), channel_id=1, source_target_pairs={{0,2},{1,3},{2,0},{3,1},{4,6},{5,7},{6,4},{7,5},{8,10},{9,11},{10,... | collective-permute-start | bytes 294920 | tf_op jit(solution)/shard_map/ppermute | solution.py:17
  185.7 4.7 %copy-start.2 = (f32[24,8,3]{0,2,1:T(4,128)S(1)}, f32[24,8,3]{0,2,1:T(4,128)}, u32[]{:S(2)}) copy-start(f32[24,8,3]{0,2,1:T(4,128)} %get-tuple-element.7) | copy-start | bytes 6916
  187.0 10.3 %all-to-all-start.1 = ((bf16[8,1,3,2048]{3,2,1,0:T(4,128)(2,1)}), bf16[8,1,3,2048]{3,2,1,0:T(4,128)(2,1)S(1)}, u32[]{:S(2)}, u32[]{:S(2)}) async-start(bf16[8,1,3,2048]{3,2,1,0:T(4,128)(2,1)} %copy.43), calls=%async_computation.1 | async-start | bytes 262144 | tf_op jit(solution)/shard_map/all_to_all | solution.py:117
  190.3 134.8 %all-reduce.5.cloned.1.call-start = ((), (), s32[]{:S(2)}) async-start(), calls=%async_computation.3 | async-start | bytes 393216 | tf_op jit(solution)/shard_map/psum | solution.py:125
Sparse Core Ops, SparseCore 0:
  34.5 131.9 all-reduce.2
  199.9 125.1 all-reduce.4
where the time goes:
time: 334 us; the launch traced here: 333 us
  waiting for transfers between devices  268 us (80%)
  starting transfers between devices  15.9 us (5%)
  between operations  13.5 us (4%)
  blocking collectives  13.4 us (4%)
  matrix products  13 us (4%)
  other arithmetic  6.89 us (2%)
    psum x1, waiting for transfers between devices, body(): summed = lax.psum(projected, ('side', 'tp'))  131 us
    psum x1, waiting for transfers between devices, body(): moe_whole = lax.psum(moe_part, ('side', 'tp'))  125 us
    all_to_all x1, blocking collectives, body(): lax.all_to_all(outgoing, 'grp', split_axis=0, concat_axis=0, tiled=True)  13.4 us
    ppermute x6, starting transfers between devices, swapped(): return lax.ppermute(value, axis, pairs)  12.4 us
    all_to_all x1, waiting for transfers between devices, body(): lax.all_to_all(produced, 'grp', split_axis=0, concat_axis=0, tiled=True)  6.8 us
  transfers between devices with their start and end apart: 9, of which 7 were waited for; matrix products, arithmetic and copies ran while one was open for 2% of the time, Pallas kernels for 0%

commit v1 on v0

v1 whole, which is shorter than its diff:
```python
import functools
import math

import jax
import jax.numpy as jnp
from jax import lax
from jax.experimental import pallas as pl
from jax.experimental.pallas import tpu as pltpu
from jax.sharding import PartitionSpec as P

HD = 128
TOPK = 8
NEG = -1e30
F32 = jnp.float32
BF16 = jnp.bfloat16
MESH = pl.DeviceIdType.MESH


def kernel(
    dims,
    len_ref,
    q_hbm,
    kv_hbm,
    ow_hbm,
    resid_hbm,
    gain_ref,
    ids_ref,
    gates_ref,
    wgu_hbm,
    wd_hbm,
    out_ref,
    q_v,
    kv_v,
    ow_v,
    res_v,
    wgu_v,
    wd_v,
    qf,
    num,
    lse,
    a_send,
    a_recv,
    b_send,
    b_recv,
    mid_all,
    d_send,
    d_recv,
    e_send,
    e_recv,
    f_send,
    f_recv,
    kv_sem,
    in_sem,
    send_sem,
    recv_sem,
):
    sides, grps, tps, parts = dims
    members = sides * tps
    rows = q_v.shape[0]
    heads = q_v.shape[1] // HD
    span = kv_v.shape[1]
    width = ow_v.shape[1]
    mine_rows = rows * heads // parts
    inner = wd_v.shape[0]
    side = lax.axis_index("side")
    grp = lax.axis_index("grp")
    tp = lax.axis_index("tp")
    member = side * tps + tp
    part = lax.rem(tp, parts)
    head_group = tp // parts

    def group_peer(d):
        other = lax.rem(member + d, members)
        return other, (other // tps, grp, lax.rem(other, tps))

    def grp_peer(d):
        other = lax.rem(grp + d, grps)
        return other, (side, other, tp)

    def part_peer(d):
        other = lax.rem(part + d, parts)
        return other, (side, grp, head_group * parts + other)

    barrier = pltpu.get_barrier_semaphore()
    for d in range(1, members):
        pl.semaphore_signal(barrier, inc=1, device_id=group_peer(d)[1], device_id_type=MESH)
    for d in range(1, grps):
        pl.semaphore_signal(barrier, inc=1, device_id=grp_peer(d)[1], device_id_type=MESH)

    q_copy = pltpu.make_async_copy(
        q_hbm.at[:, pl.ds(pl.multiple_of(head_group * heads * HD, 128), heads * HD)], q_v, in_sem.at[0]
    )
    q_copy.start()
    kv_copies = []
    chunks = kv_sem.shape[0]
    per_chunk = rows // chunks
    for c in range(chunks):
        copy = pltpu.make_async_copy(
            kv_hbm.at[pl.ds(c * per_chunk, per_chunk), 0], kv_v.at[pl.ds(c * per_chunk, per_chunk)], kv_sem.at[c]
        )
        copy.start()
        kv_copies.append(copy)
    ow_copy = pltpu.make_async_copy(ow_hbm, ow_v, in_sem.at[1])
    ow_copy.start()
    res_copy = pltpu.make_async_copy(
        resid_hbm.at[:, pl.ds(pl.multiple_of(member * 128, 128), 128)], res_v, in_sem.at[2]
    )
    res_copy.start()
    wgu_copy = pltpu.make_async_copy(wgu_hbm.at[0], wgu_v, in_sem.at[3])
    wgu_copy.start()
    wd_copy = pltpu.make_async_copy(wd_hbm.at[0], wd_v, in_sem.at[4])
    wd_copy.start()

    slots = grps * 4
    col = lax.broadcasted_iota(jnp.int32, (rows, slots), 1)
    expert = (side * grps + col // 4) * tps + tp
    ids = ids_ref[...]
    gates = gates_ref[...]
    hit = jnp.zeros((rows, slots), F32)
    gate_cols = jnp.zeros((rows, slots), F32)
    for k in range(TOPK):
        same = ids[:, k : k + 1] == expert
        hit = jnp.where(same, 1.0, hit)
        gate_cols = jnp.where(same, gates[:, k : k + 1], gate_cols)
    below = (
        lax.broadcasted_iota(jnp.int32, (rows, rows), 1) < lax.broadcasted_iota(jnp.int32, (rows, rows), 0)
    ).astype(F32)
    rank = jnp.dot(below.astype(BF16), hit.astype(BF16), preferred_element_type=F32)
    placed = jnp.where(rank == (col % 4).astype(F32), hit, 0.0)
    combine = placed * gate_cols
    combine_hi = combine.astype(BF16)
    combine_lo = (combine - combine_hi.astype(F32)).astype(BF16)

    q_copy.wait()
    for j in range(heads):
        qf[j * rows : (j + 1) * rows, :] = q_v[:, j * HD : (j + 1) * HD].astype(F32)
    first = part * span
    position = first + lax.broadcasted_iota(jnp.int32, (heads, span), 1)
    scale = 1.0 / math.sqrt(HD)
    for c in range(chunks):
        kv_copies[c].wait()
        for r in range(c * per_chunk, (c + 1) * per_chunk):
            query = qf[pl.ds(r, heads, stride=rows), :].astype(BF16)
            scores = lax.dot_general(
                query, kv_v[r, :, :HD], (((1,), (1,)), ((), ())), preferred_element_type=F32
            )
            valid = position < len_ref[r]
            scores = jnp.where(valid, scores * scale, NEG)
            top = jnp.max(scores, axis=1, keepdims=True)
            weights = jnp.where(valid, jnp.exp(scores - top), 0.0)
            total = jnp.sum(weights, axis=1, keepdims=True)
            value = jnp.dot(weights.astype(BF16), kv_v[r, :, HD:], preferred_element_type=F32)
            some = total > 0.0
            safe = jnp.where(some, total, 1.0)
            num[pl.ds(r, heads, stride=rows), :] = value * (1.0 / safe)
            lse[pl.ds(r, heads, stride=rows), :] = jnp.broadcast_to(
                jnp.where(some, top + jnp.log(safe), NEG), (heads, HD)
            )

    diagonal = lax.broadcasted_iota(jnp.int32, (mine_rows, HD), 0) == lax.broadcasted_iota(
        jnp.int32, (mine_rows, HD), 1
    )
    line = lax.broadcasted_iota(jnp.int32, (16, HD), 0)
    for p in range(parts):
        block = slice(p * mine_rows, (p + 1) * mine_rows)
        a_send[p, :mine_rows, :] = num[block, :].astype(BF16)
        stat = jnp.sum(jnp.where(diagonal, lse[block, :], 0.0), axis=0, keepdims=True)
        high = stat.astype(BF16).astype(F32)
        middle_word = (stat - high).astype(BF16).astype(F32)
        low = stat - high - middle_word
        words = jnp.where(line == 0, high, jnp.where(line == 1, middle_word, jnp.where(line == 2, low, 0.0)))
        a_send[p, mine_rows:, :] = words.astype(BF16)

    pl.semaphore_wait(barrier, members + grps - 2)

    def send(src, dst, index, device):
        pltpu.make_async_remote_copy(
            src_ref=src,
            dst_ref=dst,
            send_sem=send_sem.at[index],
            recv_sem=recv_sem.at[index],
            device_id=device,
            device_id_type=MESH,
        ).start()

    def totals(src, dst, index, device):
        return pltpu.make_async_remote_copy(
            src_ref=src,
            dst_ref=dst,
            send_sem=send_sem.at[index],
            recv_sem=recv_sem.at[index],
            device_id=device,
            device_id_type=MESH,
        )

    for d in range(1, parts):
        other, device = part_peer(d)
        send(a_send.at[other], a_recv.at[d - 1], 0, device)
    first_peer = part_peer(1)[1]
    done_a = totals(a_send.at[pl.ds(0, parts - 1)], a_recv, 0, first_peer)
    own = pl.ds(pl.multiple_of(part * mine_rows, 8), mine_rows)
    values = [num[own, :]]
    levels = [lse[own, :][:, 0:1]]
    done_a.wait_recv()
    for d in range(parts - 1):
        values.append(a_recv[d, :mine_rows, :].astype(F32))
        row = jnp.sum(a_recv[d, mine_rows:, :].astype(F32), axis=0, keepdims=True)
        levels.append(jnp.sum(jnp.where(diagonal, row, 0.0), axis=1, keepdims=True))
    peak = functools.reduce(jnp.maximum, levels)
    shares = [jnp.exp(level - peak) for level in levels]
    whole = functools.reduce(jnp.add, shares)
    merged = functools.reduce(jnp.add, [v * s for v, s in zip(values, shares)]) * (1.0 / whole)
    per_member = mine_rows // rows
    attended = jnp.concatenate(
        [merged[i * rows : (i + 1) * rows, :] for i in range(per_member)], axis=1
    ).astype(BF16)

    ow_copy.wait()
    projected = jnp.dot(attended, ow_v[...], preferred_element_type=F32)
    for j in range(members):
        b_send[j, :, :] = projected[:, j * 128 : (j + 1) * 128].astype(BF16)
    for d in range(1, members):
        other, device = group_peer(d)
        send(b_send.at[other], b_recv.at[d - 1], 1, device)
    group_first = group_peer(1)[1]
    done_b = totals(b_send.at[pl.ds(0, members - 1)], b_recv, 1, group_first)
    res_copy.wait()
    acc = res_v[...].astype(F32) + b_send[member, :, :].astype(F32)
    done_b.wait_recv()
    for d in range(members - 1):
        acc = acc + b_recv[d, :, :].astype(F32)
    mine = acc.astype(BF16)
    mid_all[member, :, :] = mine

    for d in range(1, members):
        _, device = group_peer(d)
        send(mid_all.at[member], mid_all.at[member], 2, device)
    done_c = totals(mid_all.at[pl.ds(0, members - 1)], mid_all.at[pl.ds(0, members - 1)], 2, group_first)
    done_c.wait_recv()
    square = jnp.zeros((rows, 128), F32)
    for j in range(members):
        wide = mid_all[j, :, :].astype(F32)
        square = square + wide * wide
    inv_rms = lax.rsqrt(jnp.sum(square, axis=1, keepdims=True) * (1.0 / width) + 1e-6)
    normed = jnp.concatenate(
        [(mid_all[j, :, :].astype(F32) * inv_rms * gain_ref[j : j + 1, :]).astype(BF16) for j in range(members)],
        axis=1,
    )
    chosen = lax.dot_general(
        placed.astype(BF16), normed, (((0,), (0,)), ((), ())), preferred_element_type=F32
    )

    for g in range(grps):
        d_send[g, :, :] = chosen[g * 4 : (g + 1) * 4, :].astype(BF16)
    for d in range(1, grps):
        other, device = grp_peer(d)
        send(d_send.at[other], d_recv.at[grp], 3, device)
    grp_first = grp_peer(1)[1]
    done_d = totals(d_send.at[pl.ds(0, grps - 1)], d_recv.at[pl.ds(0, grps - 1)], 3, grp_first)
    d_recv[grp, :, :] = d_send[grp, :, :]
    wgu_copy.wait()
    done_d.wait_recv()
    arrived = jnp.concatenate([d_recv[g, :, :].astype(F32) for g in range(grps)], axis=0).astype(BF16)
    both = jnp.dot(arrived, wgu_v[...], preferred_element_type=F32)
    gate = both[:, :inner]
    act = (gate / (1.0 + jnp.exp(-gate)) * both[:, inner:]).astype(BF16)
    wd_copy.wait()
    produced = jnp.dot(act, wd_v[...], preferred_element_type=F32)

    for g in range(grps):
        e_send[g, :, :] = produced[g * 4 : (g + 1) * 4, :].astype(BF16)
    for d in range(1, grps):
        other, device = grp_peer(d)
        send(e_send.at[other], e_recv.at[grp], 4, device)
    done_e = totals(e_send.at[pl.ds(0, grps - 1)], e_recv.at[pl.ds(0, grps - 1)], 4, grp_first)
    e_recv[grp, :, :] = e_send[grp, :, :]
    done_e.wait_recv()
    returned = jnp.concatenate([e_recv[g, :, :].astype(F32) for g in range(grps)], axis=0).astype(BF16)
    gated = jnp.dot(combine_hi, returned, preferred_element_type=F32) + jnp.dot(
        combine_lo, returned, preferred_element_type=F32
    )

    for j in range(members):
        f_send[j, :, :] = gated[:, j * 128 : (j + 1) * 128].astype(BF16)
    for d in range(1, members):
        other, device = group_peer(d)
        send(f_send.at[other], f_recv.at[d - 1], 5, device)
    done_f = totals(f_send.at[pl.ds(0, members - 1)], f_recv, 5, group_first)
    final = mid_all[member, :, :].astype(F32) + f_send[member, :, :].astype(F32)
    done_f.wait_recv()
    for d in range(members - 1):
        final = final + f_recv[d, :, :].astype(F32)
    out_ref[...] = final.astype(BF16)
    for done in (done_a, done_b, done_c, done_d, done_e, done_f):
        done.wait_send()


def body(queries, kv_cache, lengths, out_weight, resid, norm_gain, expert_ids, expert_gates, w_gate_up, w_down):
    sides, grps, tps = lax.axis_size("side"), lax.axis_size("grp"), lax.axis_size("tp")
    members = sides * tps
    rows = queries.shape[0]
    parts = 4
    heads = 8
    span = kv_cache.shape[2]
    width = out_weight.shape[1]
    mine_rows = rows * heads // parts
    vmem = pl.BlockSpec(memory_space=pltpu.VMEM)
    anywhere = pl.BlockSpec(memory_space=pl.ANY)
    return pl.pallas_call(
        functools.partial(kernel, (sides, grps, tps, parts)),
        out_shape=jax.ShapeDtypeStruct((rows, width // members), BF16),
        in_specs=[
            pl.BlockSpec(memory_space=pltpu.SMEM),
            anywhere,
            anywhere,
            anywhere,
            anywhere,
            vmem,
            vmem,
            vmem,
            anywhere,
            anywhere,
        ],
        out_specs=vmem,
        scratch_shapes=[
            pltpu.VMEM((rows, heads * HD), BF16),
            pltpu.VMEM((rows, span, 2 * HD), BF16),
            pltpu.VMEM(out_weight.shape, BF16),
            pltpu.VMEM((rows, 128), BF16),
            pltpu.VMEM(w_gate_up.shape[1:], BF16),
            pltpu.VMEM(w_down.shape[1:], BF16),
            pltpu.VMEM((rows * heads, HD), F32),
            pltpu.VMEM((rows * heads, HD), F32),
            pltpu.VMEM((rows * heads, HD), F32),
            pltpu.VMEM((parts, mine_rows + 16, HD), BF16),
            pltpu.VMEM((parts - 1, mine_rows + 16, HD), BF16),
            pltpu.VMEM((members, rows, 128), BF16),
            pltpu.VMEM((members - 1, rows, 128), BF16),
            pltpu.VMEM((members, rows, 128), BF16),
            pltpu.VMEM((grps, 4, width), BF16),
            pltpu.VMEM((grps, 4, width), BF16),
            pltpu.VMEM((grps, 4, width), BF16),
            pltpu.VMEM((grps, 4, width), BF16),
            pltpu.VMEM((members, rows, 128), BF16),
            pltpu.VMEM((members - 1, rows, 128), BF16),
            pltpu.SemaphoreType.DMA((4,)),
            pltpu.SemaphoreType.DMA((5,)),
            pltpu.SemaphoreType.DMA((6,)),
            pltpu.SemaphoreType.DMA((6,)),
        ],
        compiler_params=pltpu.CompilerParams(
            collective_id=0, has_side_effects=True, vmem_limit_bytes=56 * 1024 * 1024
        ),
        name="layer",
    )(
        lengths,
        queries,
        kv_cache,
        out_weight,
        resid,
        norm_gain.reshape(members, width // members),
        expert_ids,
        expert_gates,
        w_gate_up,
        w_down,
    )


def solution(mesh):
    in_specs = (
        P("grp", "side"),
        P("grp", ("side", "tp"), None, None),
        P("grp"),
        P(("side", "tp"), None),
        P("grp", None),
        P(),
        P("grp", None),
        P("grp", None),
        P(("side", "grp", "tp"), None, None),
        P(("side", "grp", "tp"), None, None),
    )
    out_specs = P("grp", ("side", "tp"))
    return jax.shard_map(body, mesh=mesh, in_specs=in_specs, out_specs=out_specs, check_vma=False)
```

time: 334 us -> 46.5 us (0.14)
  waiting for transfers between devices: 268 us -> 0 us
  Pallas kernels: 0 us -> 42.3 us
  starting transfers between devices: 15.9 us -> 0 us
  between operations: 13.5 us -> 0.01 us
  blocking collectives: 13.4 us -> 0 us
  matrix products: 13 us -> 0 us
  other arithmetic: 6.89 us -> 0 us
    psum x2 -> x0, waiting for transfers between devices: 256 us -> none  [the longest x1 131 us: body(): summed = lax.psum(projected, ('side', 'tp'))]
    pallas_call x0 -> x1, Pallas kernels: none -> 42.3 us  [body(): pl.pallas_call(functools.partial(kernel, (sides, grps, tps, parts)), out_...]
    all_to_all x1 -> x0, blocking collectives: 13.4 us -> none  [body(): lax.all_to_all(outgoing, 'grp', split_axis=0, concat_axis=0, tiled=True)]
    dot_general x7 -> x0, matrix products: 13 us -> none  [the longest x1 3.73 us: body(): jnp.einsum('gjcd,jdf->gjcf', lax.all_to_all(outgoing, 'grp', split_axis=0...]
    ppermute x6 -> x0, starting transfers between devices: 12.4 us -> none  [swapped(): return lax.ppermute(value, axis, pairs)]
    all_to_all x1 -> x0, waiting for transfers between devices: 6.8 us -> none  [body(): lax.all_to_all(produced, 'grp', split_axis=0, concat_axis=0, tiled=True)]
    ppermute x6 -> x0, waiting for transfers between devices: 4.97 us -> none  [swapped(): return lax.ppermute(value, axis, pairs)]
    all_to_all x1 -> x0, starting transfers between devices: 3.37 us -> none  [body(): lax.all_to_all(produced, 'grp', split_axis=0, concat_axis=0, tiled=True)]
  transfers between devices with their start and end apart: 9 -> 0, of which waited for: 7 -> 0; matrix products, arithmetic and copies ran while one was open for 2% -> 0% of each run, Pallas kernels for 0% -> 0%
where the time goes in v1:
time: 46.5 us; the launch traced here: 46.3 us
  Pallas kernels  42.3 us (91%)
  local copies, waits for them, and re-layouts  4 us (9%)
    pallas_call x1, Pallas kernels, body(): pl.pallas_call(functools.partial(kernel, (sides, grps, tps, parts)), out_...  42.3 us
    unnamed x3, local copies, waits for them, and re-layouts  4 us

profile of v1, /device:TPU:1, one launch (start us, length us, event | category | flops | bytes accessed | tf_op | source)
XLA Modules:
  0.0 46.3 jit_solution(16747468546886657906)
XLA Ops:
  0.0 1.4 %copy.11.ids_ref = s32[24,8]{1,0:T(8,128)} copy(s32[24,8]{0,1:T(8,128)} %param.16) | data formatting | bytes 1536 | tf_op args[6]
  1.4 1.4 %copy.12.gates_ref = f32[24,8]{1,0:T(8,128)} copy(f32[24,8]{0,1:T(8,128)} %param.17) | data formatting | bytes 1536 | tf_op args[7]
  2.7 42.3 %layer.1 = bf16[24,128]{1,0:T(8,128)(2,1)} custom-call(s32[24]{0:T(128)} %len_ref.1, bf16[24,2048]{1,0:T(8,128)(2,1)} %q_hbm.1, bf16[24,1,192,256]{3,2,1,0:T(8,128)(2,1)} %kv_hbm.1, bf16[256,2048]{1,0:T(8,128)(2,1)} %ow_hbm.1, bf16[24,2048]{1,0:T(8,128)(2,1)} %resid_hbm.1, f32[16,128]{1,0:T(8,128)} %bitcast.1, s32[24,8]{1,0:T(8,128)} %copy.11.ids_ref, ...), custom_call_target="tpu_custom_call" | custom-call | tf_op jit(solution)/shard_map/layer/pallas_call | solution.py:309
  45.0 1.3 %copy.14 = bf16[24,128]{1,0:T(8,128)(2,1)} copy(bf16[24,128]{1,0:T(8,128)(2,1)} %layer.1) | data formatting | bytes 12288

commit v2 on v1

v2 whole, which is shorter than its diff:
```python
import functools
import math

import jax
import jax.numpy as jnp
from jax import lax
from jax.experimental import pallas as pl
from jax.experimental.pallas import tpu as pltpu
from jax.sharding import PartitionSpec as P

HD = 128
TOPK = 8
SLOTS = 4
NEG = -1e30
F32 = jnp.float32
BF16 = jnp.bfloat16
MESH = pl.DeviceIdType.MESH


def kernel(
    dims,
    len_hbm,
    q_hbm,
    kv_hbm,
    ow_hbm,
    resid_hbm,
    gain_hbm,
    ids_hbm,
    gates_hbm,
    wgu_hbm,
    wd_hbm,
    out_ref,
    len_ref,
    gain_v,
    ids_v,
    gates_v,
    q_v,
    kv_v,
    ow_v,
    res_v,
    wgu_v,
    wd_v,
    qf,
    num,
    lse,
    pick,
    mix,
    a_send,
    a_recv,
    b_send,
    b_recv,
    d_send,
    d_recv,
    e_send,
    e_recv,
    small_sem,
    kv_sem,
    in_sem,
    send_sem,
    recv_sem,
):
    sides, grps, tps, parts = dims
    members = sides * tps
    experts = members * grps
    rows = q_v.shape[0]
    heads = q_v.shape[1] // HD
    span = kv_v.shape[1]
    width = ow_v.shape[1]
    mine_rows = rows * heads // parts
    inner = wd_v.shape[0]
    side = lax.axis_index("side")
    grp = lax.axis_index("grp")
    tp = lax.axis_index("tp")
    member = side * tps + tp
    part = lax.rem(tp, parts)
    head_group = tp // parts
    groups = tps // parts
    mine_expert = (side * grps + grp) * tps + tp

    grp_low = 4 if grps % 4 == 0 else grps
    grp_high = grps // grp_low
    side_at = [lax.rem(side + d, sides) for d in range(sides)]
    grp_at = {}
    for hi in range(grp_high):
        for lo in range(grp_low):
            grp_at[hi, lo] = lax.rem(grp // grp_low + hi, grp_high) * grp_low + lax.rem(
                lax.rem(grp, grp_low) + lo, grp_low
            )
    tp_at = {}
    for hi in range(groups):
        for lo in range(parts):
            tp_at[hi, lo] = lax.rem(head_group + hi, groups) * parts + lax.rem(part + lo, parts)

    def ring(d, size):
        return min(d, size - d)

    offsets = []
    for ds in range(sides):
        for gh, gl in grp_at:
            for th, tl in tp_at:
                if ds or gh or gl or th or tl:
                    far = 2 * gh + ring(gl, grp_low) + th + ring(tl, parts)
                    offsets.append((-far, ds, gh, gl, th, tl))
    offsets.sort()
    everyone = [(side_at[ds], grp_at[gh, gl], tp_at[th, tl]) for _, ds, gh, gl, th, tl in offsets]
    row_group = [
        (side_at[ds], grp, tp_at[th, tl]) for _, ds, gh, gl, th, tl in offsets if not (gh or gl)
    ]
    column = [(side, grp_at[gh, gl], tp) for _, ds, gh, gl, th, tl in offsets if not (ds or th or tl)]
    same_head = [
        (side, grp, tp_at[th, tl]) for _, ds, gh, gl, th, tl in offsets if not (ds or gh or gl or th)
    ]

    q_copy = pltpu.make_async_copy(
        q_hbm.at[:, pl.ds(pl.multiple_of(head_group * heads * HD, 128), heads * HD)], q_v, in_sem.at[0]
    )
    q_copy.start()
    len_copy = pltpu.make_async_copy(len_hbm, len_ref, small_sem.at[0])
    len_copy.start()
    kv_copies = []
    chunks = kv_sem.shape[0]
    per_chunk = rows // chunks
    for c in range(chunks):
        copy = pltpu.make_async_copy(
            kv_hbm.at[pl.ds(c * per_chunk, per_chunk), 0], kv_v.at[pl.ds(c * per_chunk, per_chunk)], kv_sem.at[c]
        )
        copy.start()
        kv_copies.append(copy)

    barrier = pltpu.get_barrier_semaphore()
    for device in column + row_group:
        pl.semaphore_signal(barrier, inc=1, device_id=device, device_id_type=MESH)

    ids_copy = pltpu.make_async_copy(ids_hbm, ids_v, small_sem.at[1])
    ids_copy.start()
    gates_copy = pltpu.make_async_copy(gates_hbm, gates_v, small_sem.at[2])
    gates_copy.start()
    gain_copy = pltpu.make_async_copy(gain_hbm, gain_v, small_sem.at[3])
    gain_copy.start()
    ow_copy = pltpu.make_async_copy(ow_hbm, ow_v, in_sem.at[1])
    ow_copy.start()
    res_copy = pltpu.make_async_copy(
        resid_hbm.at[:, pl.ds(pl.multiple_of(member * 128, 128), 128)], res_v, in_sem.at[2]
    )
    res_copy.start()
    wgu_copy = pltpu.make_async_copy(wgu_hbm.at[0], wgu_v, in_sem.at[3])
    wgu_copy.start()
    wd_copy = pltpu.make_async_copy(wd_hbm.at[0], wd_v, in_sem.at[4])
    wd_copy.start()

    ids_copy.wait()
    gates_copy.wait()
    eye = (
        lax.broadcasted_iota(jnp.int32, (TOPK, TOPK), 0) == lax.broadcasted_iota(jnp.int32, (TOPK, TOPK), 1)
    ).astype(BF16)

    def flipped(value):
        return lax.dot_general(value.astype(BF16), eye, (((0,), (0,)), ((), ())), preferred_element_type=F32)

    gates_t = gates_v[...]
    gates_high = gates_t.astype(BF16).astype(F32)
    gates_middle = (gates_t - gates_high).astype(BF16).astype(F32)
    ids = flipped(ids_v[...].astype(F32))
    gates = flipped(gates_high) + (flipped(gates_middle) + flipped(gates_t - gates_high - gates_middle))
    col = lax.broadcasted_iota(jnp.int32, (rows, experts * SLOTS), 1)
    expert = (col // SLOTS).astype(F32)
    hit = jnp.zeros((rows, experts * SLOTS), F32)
    gate_cols = jnp.zeros((rows, experts * SLOTS), F32)
    for k in range(TOPK):
        same = ids[:, k : k + 1] == expert
        hit = jnp.where(same, 1.0, hit)
        gate_cols = jnp.where(same, gates[:, k : k + 1], gate_cols)
    below = (
        lax.broadcasted_iota(jnp.int32, (rows, rows), 1) < lax.broadcasted_iota(jnp.int32, (rows, rows), 0)
    ).astype(BF16)
    rank = jnp.dot(below, hit.astype(BF16), preferred_element_type=F32)
    placed = jnp.where(rank == (col % SLOTS).astype(F32), hit, 0.0)
    same_row = (
        lax.broadcasted_iota(jnp.int32, (rows, rows), 1) == lax.broadcasted_iota(jnp.int32, (rows, rows), 0)
    ).astype(BF16)
    pick[...] = lax.dot_general(
        placed.astype(BF16), same_row, (((0,), (0,)), ((), ())), preferred_element_type=F32
    ).astype(BF16)
    combine = placed * gate_cols
    combine_high = combine.astype(BF16).astype(F32)
    mix[...] = jnp.concatenate([combine_high, combine - combine_high], axis=0).astype(BF16)

    q_copy.wait()
    for j in range(heads):
        qf[j * rows : (j + 1) * rows, :] = q_v[:, j * HD : (j + 1) * HD].astype(F32)
    len_copy.wait()
    first = part * span
    position = first + lax.broadcasted_iota(jnp.int32, (heads, span), 1)
    scale = 1.0 / math.sqrt(HD)
    for c in range(chunks):
        kv_copies[c].wait()
        for r in range(c * per_chunk, (c + 1) * per_chunk):
            query = qf[pl.ds(r, heads, stride=rows), :].astype(BF16)
            scores = lax.dot_general(
                query, kv_v[r, :, :HD], (((1,), (1,)), ((), ())), preferred_element_type=F32
            )
            valid = position < len_ref[r]
            scores = jnp.where(valid, scores * scale, NEG)
            top = jnp.max(scores, axis=1, keepdims=True)
            weights = jnp.where(valid, jnp.exp(scores - top), 0.0)
            total = jnp.sum(weights, axis=1, keepdims=True)
            value = jnp.dot(weights.astype(BF16), kv_v[r, :, HD:], preferred_element_type=F32)
            some = total > 0.0
            safe = jnp.where(some, total, 1.0)
            num[pl.ds(r, heads, stride=rows), :] = value * (1.0 / safe)
            lse[pl.ds(r, heads, stride=rows), :] = jnp.broadcast_to(
                jnp.where(some, top + jnp.log(safe), NEG), (heads, HD)
            )

    diagonal = lax.broadcasted_iota(jnp.int32, (mine_rows, HD), 0) == lax.broadcasted_iota(
        jnp.int32, (mine_rows, HD), 1
    )
    line = lax.broadcasted_iota(jnp.int32, (16, HD), 0)
    for p in range(parts):
        block = slice(p * mine_rows, (p + 1) * mine_rows)
        a_send[p, :mine_rows, :] = num[block, :].astype(BF16)
        stat = jnp.sum(jnp.where(diagonal, lse[block, :], 0.0), axis=0, keepdims=True)
        high = stat.astype(BF16).astype(F32)
        middle_word = (stat - high).astype(BF16).astype(F32)
        low = stat - high - middle_word
        words = jnp.where(line == 0, high, jnp.where(line == 1, middle_word, jnp.where(line == 2, low, 0.0)))
        a_send[p, mine_rows:, :] = words.astype(BF16)

    pl.semaphore_wait(barrier, members + grps - 2)

    def remote(src, dst, index, device):
        return pltpu.make_async_remote_copy(
            src_ref=src,
            dst_ref=dst,
            send_sem=send_sem.at[index],
            recv_sem=recv_sem.at[index],
            device_id=device,
            device_id_type=MESH,
        )

    for i, device in enumerate(same_head):
        remote(a_send.at[lax.rem(device[2], parts)], a_recv.at[i], 0, device).start()
    done_a = remote(a_send.at[pl.ds(0, parts - 1)], a_recv, 0, same_head[0])
    own = pl.ds(pl.multiple_of(part * mine_rows, 8), mine_rows)
    values = [num[own, :]]
    levels = [lse[own, :][:, 0:1]]
    done_a.wait_recv()
    for d in range(parts - 1):
        values.append(a_recv[d, :mine_rows, :].astype(F32))
        row = jnp.sum(a_recv[d, mine_rows:, :].astype(F32), axis=0, keepdims=True)
        levels.append(jnp.sum(jnp.where(diagonal, row, 0.0), axis=1, keepdims=True))
    peak = functools.reduce(jnp.maximum, levels)
    shares = [jnp.exp(level - peak) for level in levels]
    whole = functools.reduce(jnp.add, shares)
    merged = functools.reduce(jnp.add, [v * s for v, s in zip(values, shares)]) * (1.0 / whole)
    per_member = mine_rows // rows
    attended = jnp.concatenate(
        [merged[i * rows : (i + 1) * rows, :] for i in range(per_member)], axis=1
    ).astype(BF16)

    ow_copy.wait()
    projected = jnp.dot(attended, ow_v[...], preferred_element_type=F32)
    for j in range(members):
        b_send[j, :, :] = projected[:, j * 128 : (j + 1) * 128].astype(BF16)
    for i, device in enumerate(row_group):
        remote(b_send.at[device[0] * tps + device[2]], b_recv.at[i], 1, device).start()
    done_b = remote(b_send.at[pl.ds(0, members - 1)], b_recv, 1, row_group[0])
    res_copy.wait()
    acc = res_v[...].astype(F32) + b_send[member, :, :].astype(F32)
    done_b.wait_recv()
    for d in range(members - 1):
        acc = acc + b_recv[d, :, :].astype(F32)
    middle = acc.astype(BF16)

    chosen = jnp.dot(pick[...], middle, preferred_element_type=F32).astype(BF16)
    d_send[...] = chosen.reshape(experts, SLOTS, 128)
    slot = member * grps + grp
    for device in everyone:
        remote(d_send.at[(device[0] * grps + device[1]) * tps + device[2]], d_recv.at[slot], 2, device).start()
    d_recv[slot, :, :] = d_send[mine_expert, :, :]
    done_d = remote(d_send.at[pl.ds(0, experts - 1)], d_recv.at[pl.ds(0, experts - 1)], 2, everyone[0])
    gain_copy.wait()
    wgu_copy.wait()
    done_d.wait_recv()
    pieces = [
        d_recv[j * grps : (j + 1) * grps, :, :].reshape(grps * SLOTS, 128).astype(F32) for j in range(members)
    ]
    square = functools.reduce(jnp.add, [piece * piece for piece in pieces])
    inv_rms = lax.rsqrt(jnp.sum(square, axis=1, keepdims=True) * (1.0 / width) + 1e-6)
    normed = jnp.concatenate(
        [(piece * inv_rms * gain_v[j : j + 1, :]).astype(BF16) for j, piece in enumerate(pieces)], axis=1
    )
    both = jnp.dot(normed, wgu_v[...], preferred_element_type=F32)
    gate = both[:, :inner]
    act = (gate / (1.0 + jnp.exp(-gate)) * both[:, inner:]).astype(BF16)
    wd_copy.wait()
    produced = jnp.dot(act, wd_v[...], preferred_element_type=F32).astype(BF16)

    for j in range(members):
        e_send[:, j, :, :] = produced[:, j * 128 : (j + 1) * 128].reshape(grps, SLOTS, 128)
    for device in everyone:
        remote(e_send.at[device[1], device[0] * tps + device[2]], e_recv.at[mine_expert], 3, device).start()
    e_recv[mine_expert, :, :] = e_send[grp, member, :, :]
    done_e = remote(e_recv.at[pl.ds(0, experts - 1)], e_recv.at[pl.ds(0, experts - 1)], 3, everyone[0])
    done_e.wait_recv()
    returned = e_recv[...].reshape(experts * SLOTS, 128)
    gated = jnp.dot(mix[...], returned, preferred_element_type=F32)
    out_ref[...] = (middle.astype(F32) + (gated[:rows, :] + gated[rows:, :])).astype(BF16)
    for done in (done_a, done_b, done_d, done_e):
        done.wait_send()


def body(queries, kv_cache, lengths, out_weight, resid, norm_gain, expert_ids, expert_gates, w_gate_up, w_down):
    sides, grps, tps = lax.axis_size("side"), lax.axis_size("grp"), lax.axis_size("tp")
    members = sides * tps
    experts = members * grps
    rows = queries.shape[0]
    parts = 4
    heads = 8
    span = kv_cache.shape[2]
    width = out_weight.shape[1]
    mine_rows = rows * heads // parts
    anywhere = pl.BlockSpec(memory_space=pl.ANY)
    return pl.pallas_call(
        functools.partial(kernel, (sides, grps, tps, parts)),
        out_shape=jax.ShapeDtypeStruct((rows, width // members), BF16),
        in_specs=[anywhere] * 10,
        out_specs=pl.BlockSpec(memory_space=pltpu.VMEM),
        scratch_shapes=[
            pltpu.SMEM((rows,), jnp.int32),
            pltpu.VMEM((members, width // members), F32),
            pltpu.VMEM((TOPK, rows), jnp.int32),
            pltpu.VMEM((TOPK, rows), F32),
            pltpu.VMEM((rows, heads * HD), BF16),
            pltpu.VMEM((rows, span, 2 * HD), BF16),
            pltpu.VMEM(out_weight.shape, BF16),
            pltpu.VMEM((rows, 128), BF16),
            pltpu.VMEM(w_gate_up.shape[1:], BF16),
            pltpu.VMEM(w_down.shape[1:], BF16),
            pltpu.VMEM((rows * heads, HD), F32),
            pltpu.VMEM((rows * heads, HD), F32),
            pltpu.VMEM((rows * heads, HD), F32),
            pltpu.VMEM((experts * SLOTS, rows), BF16),
            pltpu.VMEM((2 * rows, experts * SLOTS), BF16),
            pltpu.VMEM((parts, mine_rows + 16, HD), BF16),
            pltpu.VMEM((parts - 1, mine_rows + 16, HD), BF16),
            pltpu.VMEM((members, rows, 128), BF16),
            pltpu.VMEM((members - 1, rows, 128), BF16),
            pltpu.VMEM((experts, SLOTS, 128), BF16),
            pltpu.VMEM((experts, SLOTS, 128), BF16),
            pltpu.VMEM((grps, members, SLOTS, 128), BF16),
            pltpu.VMEM((experts, SLOTS, 128), BF16),
            pltpu.SemaphoreType.DMA((4,)),
            pltpu.SemaphoreType.DMA((4,)),
            pltpu.SemaphoreType.DMA((5,)),
            pltpu.SemaphoreType.DMA((4,)),
            pltpu.SemaphoreType.DMA((4,)),
        ],
        compiler_params=pltpu.CompilerParams(
            collective_id=0, has_side_effects=True, vmem_limit_bytes=56 * 1024 * 1024
        ),
        name="layer",
    )(
        lengths,
        queries,
        kv_cache,
        out_weight,
        resid,
        norm_gain.reshape(members, width // members),
        expert_ids.T,
        expert_gates.T,
        w_gate_up,
        w_down,
    )


def solution(mesh):
    in_specs = (
        P("grp", "side"),
        P("grp", ("side", "tp"), None, None),
        P("grp"),
        P(("side", "tp"), None),
        P("grp", None),
        P(),
        P("grp", None),
        P("grp", None),
        P(("side", "grp", "tp"), None, None),
        P(("side", "grp", "tp"), None, None),
    )
    out_specs = P("grp", ("side", "tp"))
    return jax.shard_map(body, mesh=mesh, in_specs=in_specs, out_specs=out_specs, check_vma=False)
```

time: 46.5 us -> 39.6 us (0.85)
  Pallas kernels: 42.3 us -> 38.1 us
  local copies, waits for them, and re-layouts: 4 us -> 1.29 us
    pallas_call x1, Pallas kernels: 42.3 us -> 38.1 us  [body(): pl.pallas_call(functools.partial(kernel, (sides, grps, tps, parts)), out_...]
    unnamed x3 -> x1, local copies, waits for them, and re-layouts: 4 us -> 1.29 us
where the time goes in v2:
time: 39.6 us; the launch traced here: 39.4 us
  Pallas kernels  38.1 us (96%)
  local copies, waits for them, and re-layouts  1.29 us (3%)
    pallas_call x1, Pallas kernels, body(): pl.pallas_call(functools.partial(kernel, (sides, grps, tps, parts)), out_...  38.1 us
    unnamed x1, local copies, waits for them, and re-layouts  1.29 us

profile of v2, /device:TPU:1, one launch (start us, length us, event | category | flops | bytes accessed | tf_op | source)
XLA Modules:
  0.0 39.4 jit_solution(7886978085080107766)
XLA Ops:
  0.0 38.1 %layer.1 = bf16[24,128]{1,0:T(8,128)(2,1)} custom-call(s32[24]{0:T(128)} %len_hbm.1, bf16[24,2048]{1,0:T(8,128)(2,1)} %q_hbm.1, bf16[24,1,192,256]{3,2,1,0:T(8,128)(2,1)} %kv_hbm.1, bf16[256,2048]{1,0:T(8,128)(2,1)} %ow_hbm.1, bf16[24,2048]{1,0:T(8,128)(2,1)} %resid_hbm.1, f32[16,128]{1,0:T(8,128)} %bitcast.3, s32[8,24]{1,0:T(8,128)} %bitcast.4, ...), custom_call_target="tpu_custom_call" | custom-call | tf_op jit(solution)/shard_map/layer/pallas_call | solution.py:324
  38.1 1.3 %copy.12 = bf16[24,128]{1,0:T(8,128)(2,1)} copy(bf16[24,128]{1,0:T(8,128)(2,1)} %layer.1) | data formatting | bytes 12288

commit v3 on v2

--- a/solution.py
+++ b/solution.py
@@ -192,25 +192,45 @@
     first = part * span
     position = first + lax.broadcasted_iota(jnp.int32, (heads, span), 1)
     scale = 1.0 / math.sqrt(HD)
-    for c in range(chunks):
-        kv_copies[c].wait()
-        for r in range(c * per_chunk, (c + 1) * per_chunk):
+
+    def attend_scores(batch):
+        made = []
+        for r in batch:
             query = qf[pl.ds(r, heads, stride=rows), :].astype(BF16)
-            scores = lax.dot_general(
-                query, kv_v[r, :, :HD], (((1,), (1,)), ((), ())), preferred_element_type=F32
+            made.append(
+                lax.dot_general(query, kv_v[r, :, :HD], (((1,), (1,)), ((), ())), preferred_element_type=F32)
             )
-            valid = position < len_ref[r]
-            scores = jnp.where(valid, scores * scale, NEG)
-            top = jnp.max(scores, axis=1, keepdims=True)
-            weights = jnp.where(valid, jnp.exp(scores - top), 0.0)
-            total = jnp.sum(weights, axis=1, keepdims=True)
-            value = jnp.dot(weights.astype(BF16), kv_v[r, :, HD:], preferred_element_type=F32)
+        return made
+
+    def attend_values(batch, made):
+        valids = [position < len_ref[r] for r in batch]
+        made = [jnp.where(valid, score * scale, NEG) for valid, score in zip(valids, made)]
+        tops = [jnp.max(score, axis=1, keepdims=True) for score in made]
+        weights = [
+            jnp.where(valid, jnp.exp(score - top), 0.0) for valid, score, top in zip(valids, made, tops)
+        ]
+        totals = [jnp.sum(weight, axis=1, keepdims=True) for weight in weights]
+        results = [
+            jnp.dot(weight.astype(BF16), kv_v[r, :, HD:], preferred_element_type=F32)
+            for r, weight in zip(batch, weights)
+        ]
+        for r, top, total, value in zip(batch, tops, totals, results):
             some = total > 0.0
             safe = jnp.where(some, total, 1.0)
             num[pl.ds(r, heads, stride=rows), :] = value * (1.0 / safe)
             lse[pl.ds(r, heads, stride=rows), :] = jnp.broadcast_to(
                 jnp.where(some, top + jnp.log(safe), NEG), (heads, HD)
             )
+
+    batches = [range(c * per_chunk, (c + 1) * per_chunk) for c in range(chunks)]
+    ready = None
+    for c in range(chunks):
+        kv_copies[c].wait()
+        made = attend_scores(batches[c])
+        if ready is not None:
+            attend_values(batches[c - 1], ready)
+        ready = made
+    attend_values(batches[-1], ready)
 
     diagonal = lax.broadcasted_iota(jnp.int32, (mine_rows, HD), 0) == lax.broadcasted_iota(
         jnp.int32, (mine_rows, HD), 1
@@ -351,7 +371,7 @@
             pltpu.VMEM((grps, members, SLOTS, 128), BF16),
             pltpu.VMEM((experts, SLOTS, 128), BF16),
             pltpu.SemaphoreType.DMA((4,)),
-            pltpu.SemaphoreType.DMA((4,)),
+            pltpu.SemaphoreType.DMA((2,)),
             pltpu.SemaphoreType.DMA((5,)),
             pltpu.SemaphoreType.DMA((4,)),
             pltpu.SemaphoreType.DMA((4,)),

time: 39.6 us -> 34.4 us (0.87)
  Pallas kernels: 38.1 us -> 33 us
    pallas_call x1, Pallas kernels: 38.1 us -> 33 us  [body(): pl.pallas_call(functools.partial(kernel, (sides, grps, tps, parts)), out_...]
where the time goes in v3:
time: 34.4 us; the launch traced here: 34.3 us
  Pallas kernels  33 us (96%)
  local copies, waits for them, and re-layouts  1.29 us (4%)
    pallas_call x1, Pallas kernels, body(): pl.pallas_call(functools.partial(kernel, (sides, grps, tps, parts)), out_...  33 us
    unnamed x1, local copies, waits for them, and re-layouts  1.29 us

profile of v3, /device:TPU:1, one launch (start us, length us, event | category | flops | bytes accessed | tf_op | source)
XLA Modules:
  0.0 34.3 jit_solution(3592146666954209958)
XLA Ops:
  0.0 33.0 %layer.1 = bf16[24,128]{1,0:T(8,128)(2,1)} custom-call(s32[24]{0:T(128)} %len_hbm.1, bf16[24,2048]{1,0:T(8,128)(2,1)} %q_hbm.1, bf16[24,1,192,256]{3,2,1,0:T(8,128)(2,1)} %kv_hbm.1, bf16[256,2048]{1,0:T(8,128)(2,1)} %ow_hbm.1, bf16[24,2048]{1,0:T(8,128)(2,1)} %resid_hbm.1, f32[16,128]{1,0:T(8,128)} %bitcast.3, s32[8,24]{1,0:T(8,128)} %bitcast.4, ...), custom_call_target="tpu_custom_call" | custom-call | tf_op jit(solution)/shard_map/layer/pallas_call | solution.py:344
  33.0 1.3 %copy.12 = bf16[24,128]{1,0:T(8,128)(2,1)} copy(bf16[24,128]{1,0:T(8,128)(2,1)} %layer.1) | data formatting | bytes 12288

commit v4 on v3

--- a/solution.py
+++ b/solution.py
@@ -343,7 +343,7 @@
     anywhere = pl.BlockSpec(memory_space=pl.ANY)
     return pl.pallas_call(
         functools.partial(kernel, (sides, grps, tps, parts)),
-        out_shape=jax.ShapeDtypeStruct((rows, width // members), BF16),
+        out_shape=pltpu.VMEM((rows, width // members), BF16),
         in_specs=[anywhere] * 10,
         out_specs=pl.BlockSpec(memory_space=pltpu.VMEM),
         scratch_shapes=[

time: 34.4 us -> 31.7 us (0.922)
  Pallas kernels: 33 us -> 31 us
  local copies, waits for them, and re-layouts: 1.29 us -> 0.6 us
    pallas_call x1, Pallas kernels: 33 us -> 31 us  [body(): pl.pallas_call(functools.partial(kernel, (sides, grps, tps, parts)), out_...]
    unnamed x1, local copies, waits for them, and re-layouts: 1.29 us -> 0.6 us
where the time goes in v4:
time: 31.7 us; the launch traced here: 31.6 us
  Pallas kernels  31 us (98%)
  local copies, waits for them, and re-layouts  0.6 us (2%)
    pallas_call x1, Pallas kernels, body(): pl.pallas_call(functools.partial(kernel, (sides, grps, tps, parts)), out_...  31 us

profile of v4, /device:TPU:1, one launch (start us, length us, event | category | flops | bytes accessed | tf_op | source)
XLA Modules:
  0.0 31.6 jit_solution(2224859858338568401)
XLA Ops:
  0.0 31.0 %layer.1 = bf16[24,128]{1,0:T(8,128)(2,1)S(1)} custom-call(s32[24]{0:T(128)} %len_hbm.1, bf16[24,2048]{1,0:T(8,128)(2,1)} %q_hbm.1, bf16[24,1,192,256]{3,2,1,0:T(8,128)(2,1)} %kv_hbm.1, bf16[256,2048]{1,0:T(8,128)(2,1)} %ow_hbm.1, bf16[24,2048]{1,0:T(8,128)(2,1)} %resid_hbm.1, f32[16,128]{1,0:T(8,128)} %bitcast.3, s32[8,24]{1,0:T(8,128)} %bitcast.4, ...), custom_call_target="tpu_custom_call" | custom-call | tf_op jit(solution)/shard_map/layer/pallas_call | solution.py:344
  31.0 0.6 %copy.12 = bf16[24,128]{1,0:T(8,128)(2,1)} copy(bf16[24,128]{1,0:T(8,128)(2,1)S(1)} %layer.1) | data formatting | bytes 12288

commit v5 on v4

--- a/solution.py
+++ b/solution.py
@@ -58,6 +58,7 @@
     in_sem,
     send_sem,
     recv_sem,
+    band_sem,
 ):
     sides, grps, tps, parts = dims
     members = sides * tps
@@ -99,17 +100,38 @@
         for gh, gl in grp_at:
             for th, tl in tp_at:
                 if ds or gh or gl or th or tl:
-                    far = 2 * gh + ring(gl, grp_low) + th + ring(tl, parts)
+                    far = (1 if th else 2 * gh) + ring(gl, grp_low) + ring(tl, parts)
                     offsets.append((-far, ds, gh, gl, th, tl))
     offsets.sort()
-    everyone = [(side_at[ds], grp_at[gh, gl], tp_at[th, tl]) for _, ds, gh, gl, th, tl in offsets]
-    row_group = [
-        (side_at[ds], grp, tp_at[th, tl]) for _, ds, gh, gl, th, tl in offsets if not (gh or gl)
-    ]
-    column = [(side, grp_at[gh, gl], tp) for _, ds, gh, gl, th, tl in offsets if not (ds or th or tl)]
-    same_head = [
-        (side, grp, tp_at[th, tl]) for _, ds, gh, gl, th, tl in offsets if not (ds or gh or gl or th)
-    ]
+
+    def device_at(ds, gh, gl, th, tl):
+        return side_at[ds], grp_at[gh, gl], tp_at[th, tl]
+
+    everyone = [o[1:] for o in offsets]
+    row_group = [o for o in everyone if not (o[1] or o[2])]
+    piece_order = sorted(
+        [(ds, th, tl) for ds in range(sides) for th, tl in tp_at], key=lambda o: (ring(o[2], parts), o)
+    )
+    group_order = sorted(grp_at)
+    piece_index = {o: i for i, o in enumerate(piece_order)}
+    group_index = {o: i for i, o in enumerate(group_order)}
+    piece_member = [side_at[ds] * tps + tp_at[th, tl] for ds, th, tl in piece_order]
+    bands = sorted({ring(o[2], parts) for o in piece_order})
+    band_pieces = {b: [i for i, o in enumerate(piece_order) if ring(o[2], parts) == b] for b in bands}
+
+    def close(ds, gh, gl, th, tl):
+        if gh:
+            return th and not (ds or tl)
+        if gl:
+            return not (ds or th or tl)
+        return not (tl and (ds or th))
+
+    near = [o for o in everyone if close(*o)]
+    same_head = [device_at(*o) for o in everyone if not (o[0] or o[1] or o[2] or o[3])]
+
+    barrier = pltpu.get_barrier_semaphore()
+    for o in near:
+        pl.semaphore_signal(barrier, inc=1, device_id=device_at(*o), device_id_type=MESH)
 
     q_copy = pltpu.make_async_copy(
         q_hbm.at[:, pl.ds(pl.multiple_of(head_group * heads * HD, 128), heads * HD)], q_v, in_sem.at[0]
@@ -127,10 +149,6 @@
         copy.start()
         kv_copies.append(copy)
 
-    barrier = pltpu.get_barrier_semaphore()
-    for device in column + row_group:
-        pl.semaphore_signal(barrier, inc=1, device_id=device, device_id_type=MESH)
-
     ids_copy = pltpu.make_async_copy(ids_hbm, ids_v, small_sem.at[1])
     ids_copy.start()
     gates_copy = pltpu.make_async_copy(gates_hbm, gates_v, small_sem.at[2])
@@ -138,15 +156,13 @@
     gain_copy = pltpu.make_async_copy(gain_hbm, gain_v, small_sem.at[3])
     gain_copy.start()
     ow_copy = pltpu.make_async_copy(ow_hbm, ow_v, in_sem.at[1])
+    wgu_copy = pltpu.make_async_copy(wgu_hbm.at[0], wgu_v, in_sem.at[3])
+    wd_copy = pltpu.make_async_copy(wd_hbm.at[0], wd_v, in_sem.at[4])
     ow_copy.start()
     res_copy = pltpu.make_async_copy(
         resid_hbm.at[:, pl.ds(pl.multiple_of(member * 128, 128), 128)], res_v, in_sem.at[2]
     )
     res_copy.start()
-    wgu_copy = pltpu.make_async_copy(wgu_hbm.at[0], wgu_v, in_sem.at[3])
-    wgu_copy.start()
-    wd_copy = pltpu.make_async_copy(wd_hbm.at[0], wd_v, in_sem.at[4])
-    wd_copy.start()
 
     ids_copy.wait()
     gates_copy.wait()
@@ -246,21 +262,24 @@
         words = jnp.where(line == 0, high, jnp.where(line == 1, middle_word, jnp.where(line == 2, low, 0.0)))
         a_send[p, mine_rows:, :] = words.astype(BF16)
 
-    pl.semaphore_wait(barrier, members + grps - 2)
-
-    def remote(src, dst, index, device):
+    pl.semaphore_wait(barrier, len(near))
+
+    def remote(src, dst, sent, received, device):
         return pltpu.make_async_remote_copy(
             src_ref=src,
             dst_ref=dst,
-            send_sem=send_sem.at[index],
-            recv_sem=recv_sem.at[index],
+            send_sem=sent,
+            recv_sem=received,
             device_id=device,
             device_id_type=MESH,
         )
 
     for i, device in enumerate(same_head):
-        remote(a_send.at[lax.rem(device[2], parts)], a_recv.at[i], 0, device).start()
-    done_a = remote(a_send.at[pl.ds(0, parts - 1)], a_recv, 0, same_head[0])
+        remote(a_send.at[lax.rem(device[2], parts)], a_recv.at[i], send_sem.at[0], recv_sem.at[0], device).start()
+    done_a = remote(a_send.at[pl.ds(0, parts - 1)], a_recv, send_sem.at[0], recv_sem.at[0], same_head[0])
+    for i, block in enumerate(piece_member):
+        there = pl.ds(pl.multiple_of(block * 128, 128), 128)
+        pltpu.make_async_copy(wgu_hbm.at[0, there, :], wgu_v.at[pl.ds(i * 128, 128), :], in_sem.at[3]).start()
     own = pl.ds(pl.multiple_of(part * mine_rows, 8), mine_rows)
     values = [num[own, :]]
     levels = [lse[own, :][:, 0:1]]
@@ -282,9 +301,15 @@
     projected = jnp.dot(attended, ow_v[...], preferred_element_type=F32)
     for j in range(members):
         b_send[j, :, :] = projected[:, j * 128 : (j + 1) * 128].astype(BF16)
-    for i, device in enumerate(row_group):
-        remote(b_send.at[device[0] * tps + device[2]], b_recv.at[i], 1, device).start()
-    done_b = remote(b_send.at[pl.ds(0, members - 1)], b_recv, 1, row_group[0])
+    for i, o in enumerate(row_group):
+        device = device_at(*o)
+        remote(b_send.at[device[0] * tps + device[2]], b_recv.at[i], send_sem.at[1], recv_sem.at[1], device).start()
+    done_b = remote(
+        b_send.at[pl.ds(0, members - 1)], b_recv, send_sem.at[1], recv_sem.at[1], device_at(*row_group[0])
+    )
+    for i, block in enumerate(piece_member):
+        there = pl.ds(pl.multiple_of(block * 128, 128), 128)
+        pltpu.make_async_copy(wd_hbm.at[0, :, there], wd_v.at[:, pl.ds(i * 128, 128)], in_sem.at[4]).start()
     res_copy.wait()
     acc = res_v[...].astype(F32) + b_send[member, :, :].astype(F32)
     done_b.wait_recv()
@@ -294,34 +319,65 @@
 
     chosen = jnp.dot(pick[...], middle, preferred_element_type=F32).astype(BF16)
     d_send[...] = chosen.reshape(experts, SLOTS, 128)
-    slot = member * grps + grp
-    for device in everyone:
-        remote(d_send.at[(device[0] * grps + device[1]) * tps + device[2]], d_recv.at[slot], 2, device).start()
-    d_recv[slot, :, :] = d_send[mine_expert, :, :]
-    done_d = remote(d_send.at[pl.ds(0, experts - 1)], d_recv.at[pl.ds(0, experts - 1)], 2, everyone[0])
+    some_device = device_at(*everyone[0])
+    for ds, gh, gl, th, tl in everyone:
+        device = device_at(ds, gh, gl, th, tl)
+        slot = piece_index[ds, th, (parts - tl) % parts] * grps + group_index[gh, (grp_low - gl) % grp_low]
+        remote(
+            d_send.at[(device[0] * grps + device[1]) * tps + device[2]],
+            d_recv.at[slot],
+            send_sem.at[2],
+            band_sem.at[ring(tl, parts)],
+            device,
+        ).start()
+    d_recv[0, :, :] = d_send[mine_expert, :, :]
     gain_copy.wait()
     wgu_copy.wait()
-    done_d.wait_recv()
-    pieces = [
-        d_recv[j * grps : (j + 1) * grps, :, :].reshape(grps * SLOTS, 128).astype(F32) for j in range(members)
-    ]
-    square = functools.reduce(jnp.add, [piece * piece for piece in pieces])
+    both = None
+    square = None
+    for band in bands:
+        members_in = band_pieces[band]
+        count = len(members_in) * grps - (1 if band == 0 else 0)
+        some = pl.ds(0, count)
+        remote(d_recv.at[some], d_recv.at[some], send_sem.at[2], band_sem.at[band], some_device).wait_recv()
+        inputs = []
+        for i in members_in:
+            piece = d_recv[i * grps : (i + 1) * grps, :, :].reshape(grps * SLOTS, 128).astype(F32)
+            square = piece * piece if square is None else square + piece * piece
+            inputs.append((piece * gain_v[pl.ds(piece_member[i], 1), :]).astype(BF16))
+        partial = jnp.dot(
+            jnp.concatenate(inputs, axis=1),
+            wgu_v[members_in[0] * 128 : (members_in[-1] + 1) * 128, :],
+            preferred_element_type=F32,
+        )
+        both = partial if both is None else both + partial
+    done_d = remote(
+        d_send.at[pl.ds(0, experts - 1)], d_recv.at[pl.ds(0, experts - 1)], send_sem.at[2], band_sem.at[0], some_device
+    )
     inv_rms = lax.rsqrt(jnp.sum(square, axis=1, keepdims=True) * (1.0 / width) + 1e-6)
-    normed = jnp.concatenate(
-        [(piece * inv_rms * gain_v[j : j + 1, :]).astype(BF16) for j, piece in enumerate(pieces)], axis=1
-    )
-    both = jnp.dot(normed, wgu_v[...], preferred_element_type=F32)
+    both = both * inv_rms
     gate = both[:, :inner]
     act = (gate / (1.0 + jnp.exp(-gate)) * both[:, inner:]).astype(BF16)
     wd_copy.wait()
-    produced = jnp.dot(act, wd_v[...], preferred_element_type=F32).astype(BF16)
-
-    for j in range(members):
-        e_send[:, j, :, :] = produced[:, j * 128 : (j + 1) * 128].reshape(grps, SLOTS, 128)
-    for device in everyone:
-        remote(e_send.at[device[1], device[0] * tps + device[2]], e_recv.at[mine_expert], 3, device).start()
-    e_recv[mine_expert, :, :] = e_send[grp, member, :, :]
-    done_e = remote(e_recv.at[pl.ds(0, experts - 1)], e_recv.at[pl.ds(0, experts - 1)], 3, everyone[0])
+
+    for band in reversed(bands):
+        low, high = band_pieces[band][0], band_pieces[band][-1] + 1
+        produced = jnp.dot(act, wd_v[:, low * 128 : high * 128], preferred_element_type=F32).astype(BF16)
+        for p in range(low, high):
+            e_send[:, p, :, :] = produced[:, (p - low) * 128 : (p - low + 1) * 128].reshape(grps, SLOTS, 128)
+        for ds, gh, gl, th, tl in everyone:
+            p = piece_index[ds, th, tl]
+            if low <= p < high:
+                remote(
+                    e_send.at[group_index[gh, gl], p],
+                    e_recv.at[mine_expert],
+                    send_sem.at[3],
+                    recv_sem.at[2],
+                    device_at(ds, gh, gl, th, tl),
+                ).start()
+    e_recv[mine_expert, :, :] = e_send[0, 0, :, :]
+    some = pl.ds(0, experts - 1)
+    done_e = remote(e_recv.at[some], e_recv.at[some], send_sem.at[3], recv_sem.at[2], some_device)
     done_e.wait_recv()
     returned = e_recv[...].reshape(experts * SLOTS, 128)
     gated = jnp.dot(mix[...], returned, preferred_element_type=F32)
@@ -374,7 +430,8 @@
             pltpu.SemaphoreType.DMA((2,)),
             pltpu.SemaphoreType.DMA((5,)),
             pltpu.SemaphoreType.DMA((4,)),
-            pltpu.SemaphoreType.DMA((4,)),
+            pltpu.SemaphoreType.DMA((3,)),
+            pltpu.SemaphoreType.DMA((3,)),
         ],
         compiler_params=pltpu.CompilerParams(
             collective_id=0, has_side_effects=True, vmem_limit_bytes=56 * 1024 * 1024

time: 31.7 us -> 31.3 us (0.987)
  Pallas kernels: 31 us -> 30.6 us
    pallas_call x1, Pallas kernels: 31 us -> 30.6 us  [body(): pl.pallas_call(functools.partial(kernel, (sides, grps, tps, parts)), out_...]
where the time goes in v5:
time: 31.3 us; the launch traced here: 31.2 us
  Pallas kernels  30.6 us (98%)
  local copies, waits for them, and re-layouts  0.6 us (2%)
    pallas_call x1, Pallas kernels, body(): pl.pallas_call(functools.partial(kernel, (sides, grps, tps, parts)), out_...  30.6 us

profile of v5, /device:TPU:1, one launch (start us, length us, event | category | flops | bytes accessed | tf_op | source)
XLA Modules:
  0.0 31.2 jit_solution(5317355788126591087)
XLA Ops:
  0.0 30.6 %layer.1 = bf16[24,128]{1,0:T(8,128)(2,1)S(1)} custom-call(s32[24]{0:T(128)} %len_hbm.1, bf16[24,2048]{1,0:T(8,128)(2,1)} %q_hbm.1, bf16[24,1,192,256]{3,2,1,0:T(8,128)(2,1)} %kv_hbm.1, bf16[256,2048]{1,0:T(8,128)(2,1)} %ow_hbm.1, bf16[24,2048]{1,0:T(8,128)(2,1)} %resid_hbm.1, f32[16,128]{1,0:T(8,128)} %bitcast.3, s32[8,24]{1,0:T(8,128)} %bitcast.4, ...), custom_call_target="tpu_custom_call" | custom-call | tf_op jit(solution)/shard_map/layer/pallas_call | solution.py:400
  30.6 0.6 %copy.12 = bf16[24,128]{1,0:T(8,128)(2,1)} copy(bf16[24,128]{1,0:T(8,128)(2,1)S(1)} %layer.1) | data formatting | bytes 12288

commit v6 on v5

--- a/solution.py
+++ b/solution.py
@@ -59,6 +59,7 @@
     send_sem,
     recv_sem,
     band_sem,
+    hello_sem,
 ):
     sides, grps, tps, parts = dims
     members = sides * tps
@@ -121,7 +122,7 @@
 
     def close(ds, gh, gl, th, tl):
         if gh:
-            return th and not (ds or tl)
+            return th and not (ds or tl) and gl != grp_low // 2
         if gl:
             return not (ds or th or tl)
         return not (tl and (ds or th))
@@ -251,7 +252,7 @@
     diagonal = lax.broadcasted_iota(jnp.int32, (mine_rows, HD), 0) == lax.broadcasted_iota(
         jnp.int32, (mine_rows, HD), 1
     )
-    line = lax.broadcasted_iota(jnp.int32, (16, HD), 0)
+    line = lax.broadcasted_iota(jnp.int32, (8, HD), 0)
     for p in range(parts):
         block = slice(p * mine_rows, (p + 1) * mine_rows)
         a_send[p, :mine_rows, :] = num[block, :].astype(BF16)
@@ -276,6 +277,7 @@
 
     for i, device in enumerate(same_head):
         remote(a_send.at[lax.rem(device[2], parts)], a_recv.at[i], send_sem.at[0], recv_sem.at[0], device).start()
+    pl.semaphore_signal(hello_sem, inc=1, device_id=device_at(0, 1, 0, 1, 0), device_id_type=MESH)
     done_a = remote(a_send.at[pl.ds(0, parts - 1)], a_recv, send_sem.at[0], recv_sem.at[0], same_head[0])
     for i, block in enumerate(piece_member):
         there = pl.ds(pl.multiple_of(block * 128, 128), 128)
@@ -284,6 +286,7 @@
     values = [num[own, :]]
     levels = [lse[own, :][:, 0:1]]
     done_a.wait_recv()
+    pl.semaphore_wait(hello_sem, 1)
     for d in range(parts - 1):
         values.append(a_recv[d, :mine_rows, :].astype(F32))
         row = jnp.sum(a_recv[d, mine_rows:, :].astype(F32), axis=0, keepdims=True)
@@ -298,12 +301,24 @@
     ).astype(BF16)
 
     ow_copy.wait()
-    projected = jnp.dot(attended, ow_v[...], preferred_element_type=F32)
-    for j in range(members):
-        b_send[j, :, :] = projected[:, j * 128 : (j + 1) * 128].astype(BF16)
-    for i, o in enumerate(row_group):
-        device = device_at(*o)
-        remote(b_send.at[device[0] * tps + device[2]], b_recv.at[i], send_sem.at[1], recv_sem.at[1], device).start()
+    for band in reversed(bands):
+        peers = [(i, o) for i, o in enumerate(row_group) if ring(o[4], parts) == band]
+        blocks = [device_at(*o) for _, o in peers]
+        pieces = [
+            jnp.dot(
+                attended,
+                ow_v[:, pl.ds(pl.multiple_of((device[0] * tps + device[2]) * 128, 128), 128)],
+                preferred_element_type=F32,
+            )
+            for device in blocks
+        ]
+        for (i, _), piece in zip(peers, pieces):
+            b_send[i, :, :] = piece.astype(BF16)
+        for (i, _), device in zip(peers, blocks):
+            remote(b_send.at[i], b_recv.at[i], send_sem.at[1], recv_sem.at[1], device).start()
+    kept = jnp.dot(
+        attended, ow_v[:, pl.ds(pl.multiple_of(member * 128, 128), 128)], preferred_element_type=F32
+    )
     done_b = remote(
         b_send.at[pl.ds(0, members - 1)], b_recv, send_sem.at[1], recv_sem.at[1], device_at(*row_group[0])
     )
@@ -311,7 +326,7 @@
         there = pl.ds(pl.multiple_of(block * 128, 128), 128)
         pltpu.make_async_copy(wd_hbm.at[0, :, there], wd_v.at[:, pl.ds(i * 128, 128)], in_sem.at[4]).start()
     res_copy.wait()
-    acc = res_v[...].astype(F32) + b_send[member, :, :].astype(F32)
+    acc = res_v[...].astype(F32) + kept
     done_b.wait_recv()
     for d in range(members - 1):
         acc = acc + b_recv[d, :, :].astype(F32)
@@ -418,8 +433,8 @@
             pltpu.VMEM((rows * heads, HD), F32),
             pltpu.VMEM((experts * SLOTS, rows), BF16),
             pltpu.VMEM((2 * rows, experts * SLOTS), BF16),
-            pltpu.VMEM((parts, mine_rows + 16, HD), BF16),
-            pltpu.VMEM((parts - 1, mine_rows + 16, HD), BF16),
+            pltpu.VMEM((parts, mine_rows + 8, HD), BF16),
+            pltpu.VMEM((parts - 1, mine_rows + 8, HD), BF16),
             pltpu.VMEM((members, rows, 128), BF16),
             pltpu.VMEM((members - 1, rows, 128), BF16),
             pltpu.VMEM((experts, SLOTS, 128), BF16),
@@ -432,6 +447,7 @@
             pltpu.SemaphoreType.DMA((4,)),
             pltpu.SemaphoreType.DMA((3,)),
             pltpu.SemaphoreType.DMA((3,)),
+            pltpu.SemaphoreType.REGULAR,
         ],
         compiler_params=pltpu.CompilerParams(
             collective_id=0, has_side_effects=True, vmem_limit_bytes=56 * 1024 * 1024

time: 31.3 us -> 31 us (level)
  no operation moved by 1% of the time
where the time goes in v6:
time: 31 us; the launch traced here: 30.9 us
  Pallas kernels  30.3 us (98%)
  local copies, waits for them, and re-layouts  0.6 us (2%)
    pallas_call x1, Pallas kernels, body(): pl.pallas_call(functools.partial(kernel, (sides, grps, tps, parts)), out_...  30.3 us

profile of v6, /device:TPU:1, one launch (start us, length us, event | category | flops | bytes accessed | tf_op | source)
XLA Modules:
  0.0 30.9 jit_solution(9086592268101071919)
XLA Ops:
  0.0 30.3 %layer.1 = bf16[24,128]{1,0:T(8,128)(2,1)S(1)} custom-call(s32[24]{0:T(128)} %len_hbm.1, bf16[24,2048]{1,0:T(8,128)(2,1)} %q_hbm.1, bf16[24,1,192,256]{3,2,1,0:T(8,128)(2,1)} %kv_hbm.1, bf16[256,2048]{1,0:T(8,128)(2,1)} %ow_hbm.1, bf16[24,2048]{1,0:T(8,128)(2,1)} %resid_hbm.1, f32[16,128]{1,0:T(8,128)} %bitcast.3, s32[8,24]{1,0:T(8,128)} %bitcast.4, ...), custom_call_target="tpu_custom_call" | custom-call | tf_op jit(solution)/shard_map/layer/pallas_call | solution.py:415
  30.3 0.6 %copy.12 = bf16[24,128]{1,0:T(8,128)(2,1)} copy(bf16[24,128]{1,0:T(8,128)(2,1)S(1)} %layer.1) | data formatting | bytes 12288

commit v7 on v6

--- a/solution.py
+++ b/solution.py
@@ -393,12 +393,13 @@
     e_recv[mine_expert, :, :] = e_send[0, 0, :, :]
     some = pl.ds(0, experts - 1)
     done_e = remote(e_recv.at[some], e_recv.at[some], send_sem.at[3], recv_sem.at[2], some_device)
+    for done in (done_a, done_b, done_d):
+        done.wait_send()
     done_e.wait_recv()
     returned = e_recv[...].reshape(experts * SLOTS, 128)
     gated = jnp.dot(mix[...], returned, preferred_element_type=F32)
     out_ref[...] = (middle.astype(F32) + (gated[:rows, :] + gated[rows:, :])).astype(BF16)
-    for done in (done_a, done_b, done_d, done_e):
-        done.wait_send()
+    done_e.wait_send()
 
 
 def body(queries, kv_cache, lengths, out_weight, resid, norm_gain, expert_ids, expert_gates, w_gate_up, w_down):
@@ -442,7 +443,7 @@
             pltpu.VMEM((grps, members, SLOTS, 128), BF16),
             pltpu.VMEM((experts, SLOTS, 128), BF16),
             pltpu.SemaphoreType.DMA((4,)),
-            pltpu.SemaphoreType.DMA((2,)),
+            pltpu.SemaphoreType.DMA((3,)),
             pltpu.SemaphoreType.DMA((5,)),
             pltpu.SemaphoreType.DMA((4,)),
             pltpu.SemaphoreType.DMA((3,)),

time: 31 us -> 31 us (level)
  no operation moved by 1% of the time
where the time goes in v7:
time: 31 us; the launch traced here: 30.9 us
  Pallas kernels  30.3 us (98%)
  local copies, waits for them, and re-layouts  0.6 us (2%)
    pallas_call x1, Pallas kernels, body(): pl.pallas_call(functools.partial(kernel, (sides, grps, tps, parts)), out_...  30.3 us

profile of v7, /device:TPU:1, one launch (start us, length us, event | category | flops | bytes accessed | tf_op | source)
XLA Modules:
  0.0 30.9 jit_solution(1210325868044613217)
XLA Ops:
  0.0 30.3 %layer.1 = bf16[24,128]{1,0:T(8,128)(2,1)S(1)} custom-call(s32[24]{0:T(128)} %len_hbm.1, bf16[24,2048]{1,0:T(8,128)(2,1)} %q_hbm.1, bf16[24,1,192,256]{3,2,1,0:T(8,128)(2,1)} %kv_hbm.1, bf16[256,2048]{1,0:T(8,128)(2,1)} %ow_hbm.1, bf16[24,2048]{1,0:T(8,128)(2,1)} %resid_hbm.1, f32[16,128]{1,0:T(8,128)} %bitcast.3, s32[8,24]{1,0:T(8,128)} %bitcast.4, ...), custom_call_target="tpu_custom_call" | custom-call | tf_op jit(solution)/shard_map/layer/pallas_call | solution.py:416
  30.3 0.6 %copy.12 = bf16[24,128]{1,0:T(8,128)(2,1)} copy(bf16[24,128]{1,0:T(8,128)(2,1)S(1)} %layer.1) | data formatting | bytes 12288
